TPU v7x, 32 devices: a whole 2x2x4 slice. The times are simulated.
32 devices in a mesh: row: 4 (over z), col: 8 (over y, x, core).
Axes of the slice: x: 2, y: 2, z: 4, core: 2. Of those that a mesh axis runs over, the one named last changes fastest.
Arguments:
- integrals: bfloat16 [5120, 5120], P('row', 'col'), may hold values from -6 to 6
- amplitudes: bfloat16 [5120, 4096], P('row', 'col'), may hold values from -0.078125 to 0.078125
- int_shape: int32 [20, 20], P('row'), may hold values 0 or 1
- amp_shape: int32 [20, 16], P(None, 'col'), may hold values 0 or 1
Outputs:
- ladder: bfloat16 [5120, 4096], P('row', 'col')
All inputs are finite; a program needn't handle non-finite values. No bound on the sum of `int_shape` or of `amp_shape` on one device may be relied on, other than what follows from the above.
Results may differ from a plain program's by a relative error of at most 0.001.
Values may be sent and summed in bfloat16 or wider, within the bound.
A program may use at most 192 MiB of HBM per device.

v0:
```python
import jax
import jax.numpy as jnp
from jax import lax
from jax.sharding import PartitionSpec as P

TILE = 256


def expand_shape(shape_mask):
    return jnp.repeat(jnp.repeat(shape_mask, TILE, axis=0), TILE, axis=1).astype(jnp.bfloat16)


def per_device(integrals, amplitudes, int_shape, amp_shape):
    int_mask = expand_shape(int_shape)
    amp_mask = expand_shape(amp_shape)
    whole_amp = lax.all_gather(amplitudes, "row", axis=0, tiled=True) * amp_mask
    left = lax.all_gather(integrals, "col", axis=1, tiled=True) * int_mask
    total = jnp.dot(left, whole_amp, preferred_element_type=jnp.float32)
    return total.astype(jnp.bfloat16)


def solution(mesh):
    in_specs = (P("row", "col"), P("row", "col"), P("row", None), P(None, "col"))
    out_specs = P("row", "col")
    return jax.shard_map(
        per_device, mesh=mesh, in_specs=in_specs, out_specs=out_specs, check_vma=False
    )
```

profile of v0, /device:TPU:0, one launch (start us, length us, event | category | flops | bytes accessed | tf_op | source)
XLA Modules:
  0.0 208.1 jit_solution(10868750387574708260)
XLA Ops:
  6.5 0.0 copy-start
  6.5 0.0 copy-start.1
  6.5 0.0 all-gather.3.cloned.1.call-start
  6.5 3.6 %copy.9 = bf16[1280,640]{0,1:T(8,128)(2,1)} copy(bf16[1280,640]{1,0:T(8,128)(2,1)} %param.4) | data formatting | bytes 3276800 | tf_op args[0]
  10.1 0.0 all-gather.3.cloned.1.call-update
  10.1 0.0 all-gather.5.cloned.1.call-start
  10.2 0.7 all-gather.5.cloned.1.call-update
  10.9 0.0 copy-done
  10.9 0.1 copy.10
  11.0 0.1 broadcast_bitcast_fusion
  11.2 0.0 copy-done.1
  11.2 0.1 copy.11
  11.3 0.2 broadcast_in_dim.14
  11.5 6.2 %broadcast_in_dim.15 = bf16[5120,2,256]{2,1,0:T(2,128)(2,1)S(1)} broadcast(bf16[5120,2]{1,0:T(8,128)(2,1)S(1)} %bitcast.14), dimensions={0,1} | broadcast | bytes 5263360 | tf_op jit(solution)/shard_map/broadcast_in_dim | solution.py:10
  17.6 3.5 %copy.13 = bf16[640,8,2,256]{3,1,2,0:T(8,128)(2,1)} copy(bf16[640,8,2,256]{3,2,1,0:T(2,128)(2,1)S(1)} %bitcast.12) | data formatting | bytes 10485760
  21.2 66.0 %all-gather.3.cloned.1.call-done = bf16[1280,5120]{0,1:T(8,128)(2,1)} async-done(((bf16[1280,640]{0,1:T(8,128)(2,1)}), bf16[1280,5120]{0,1:T(8,128)(2,1)}) %all-gather.3.cloned.1.call-update) | async-done | bytes 13107216 | tf_op jit(solution)/shard_map/all_gather | solution.py:17
  87.2 11.5 %bitcast_multiply_fusion = bf16[1280,5120]{0,1:T(8,128)(2,1)} fusion(bf16[1280,5120]{0,1:T(8,128)(2,1)} %all-gather.3.cloned.1.call-done, bf16[1280,20]{0,1:T(8,128)(2,1)S(1)} %bitcast.16), kind=kLoop, calls=%fused_computation | loop fusion | flops 6553600 | bytes 26265600 | tf_op jit(solution)/shard_map/mul | solution.py:17
  98.7 88.1 %all-gather.5.cloned.1.call-done = bf16[5120,512]{1,0:T(8,128)(2,1)} async-done(((bf16[1280,512]{1,0:T(8,128)(2,1)}), bf16[5120,512]{1,0:T(8,128)(2,1)}) %all-gather.5.cloned.1.call-update) | async-done | bytes 5242896 | tf_op jit(solution)/shard_map/all_gather | solution.py:16
  186.9 14.4 %fusion.2 = bf16[1280,512]{1,0:T(8,128)(2,1)} fusion(bf16[1280,5120]{0,1:T(8,128)(2,1)} %bitcast_multiply_fusion, bf16[5120,512]{1,0:T(8,128)(2,1)} %all-gather.5.cloned.1.call-done, bf16[5120,512]{1,0:T(8,128)(2,1)} %bitcast.13), kind=kOutput, calls=%fused_computation.3 | convolution fusion | flops 6714163200 | bytes 24903680 | tf_op jit(solution)/shard_map/dot_general | solution.py:18
  (4 shorter events, 0.0 us)
Async XLA Ops:
  6.5 4.4 %copy-start = (s32[5,20]{1,0:T(8,128)S(1)}, s32[5,20]{1,0:T(8,128)}, u32[]{:S(2)}) copy-start(s32[5,20]{1,0:T(8,128)} %param.6) | copy-start | bytes 1204
  6.5 4.6 %copy-start.1 = (s32[20,2]{0,1:T(2,128)S(1)}, s32[20,2]{0,1:T(2,128)}, u32[]{:S(2)}) copy-start(s32[20,2]{0,1:T(2,128)} %param.7) | copy-start | bytes 484
  6.5 80.7 %all-gather.3.cloned.1.call-start = ((), (), s32[]{:S(2)}) async-start(), calls=%async_computation | async-start | bytes 14745600 | tf_op jit(solution)/shard_map/all_gather | solution.py:17
  10.1 176.7 %all-gather.5.cloned.1.call-start = ((), (), s32[]{:S(2)}) async-start(), calls=%async_computation.1 | async-start | bytes 6553600 | tf_op jit(solution)/shard_map/all_gather | solution.py:16
Sparse Core Ops, SparseCore 0:
  10.3 76.9 all-gather.2
  88.8 98.0 all-gather.4
where the time goes:
time: 208 us
  waiting for transfers between devices  155 us (75%)
  matrix products  14.4 us (7%)
  local copies, waits for them, and re-layouts  13.8 us (7%)
  between operations  13.5 us (6%)
  other arithmetic  11.5 us (6%)
    all_gather x1, waiting for transfers between devices, per_device(): whole_amp = lax.all_gather(amplitudes, 'row', axis=0, tiled=True) * amp_mask  88.1 us
    all_gather x1, waiting for transfers between devices, per_device(): left = lax.all_gather(integrals, 'col', axis=1, tiled=True) * int_mask  66 us
    dot_general x1, matrix products, per_device(): total = jnp.dot(left, whole_amp, preferred_element_type=jnp.float32)  14.4 us
    mul x1, other arithmetic, per_device(): left = lax.all_gather(integrals, 'col', axis=1, tiled=True) * int_mask  11.5 us
    unnamed x9, local copies, waits for them, and re-layouts  7.24 us
    broadcast_in_dim x1, local copies, waits for them, and re-layouts, expand_shape(): jnp.repeat(jnp.repeat(shape_mask, TILE, axis=0), TILE, axis=1)  6.16 us
  transfers between devices with their start and end apart: 2, of which 2 were waited for; matrix products, arithmetic and copies ran while one was open for 10% of the time, Pallas kernels for 0%

commit v1 on v0

v1 whole, which is shorter than its diff:
```python
import functools

import jax
import jax.numpy as jnp
from jax import lax
from jax.experimental import pallas as pl
from jax.experimental.pallas import tpu as pltpu
from jax.sharding import PartitionSpec as P

TILE = 256
CORES = 2
MESH = pl.DeviceIdType.MESH


class Plan:
    def __init__(self, n_row, n_col, rows, i_cols, a_rows, a_cols):
        self.R, self.C = n_row, n_col
        self.G = n_col // CORES
        self.nb = self.G.bit_length() - 1
        assert self.G == 1 << self.nb and self.G == n_row
        assert a_rows == i_cols * CORES and a_rows % TILE == 0 and rows % TILE == 0
        self.rows, self.i_cols, self.a_rows, self.a_cols = rows, i_cols, a_rows, a_cols
        self.RT, self.KT, self.QT = rows // TILE, a_rows // TILE, a_cols // TILE
        self.piece = {r: (r * self.nb) // self.RT for r in range(self.RT)}

    def dim(self, r, t):
        return (self.piece[r] + t) % self.nb

    def known(self, r, t):
        masks = [0]
        for u in range(t):
            masks += [m ^ (1 << self.dim(r, u)) for m in masks]
        return masks

    def sends(self, d):
        items = []
        for r in range(self.RT):
            for t in range(self.nb):
                if self.dim(r, t) == d:
                    items += [(t, m, r) for m in self.known(r, t)]
        return sorted(items, key=lambda i: (i[0], bin(i[1]).count("1"), i[2]))

    def events(self):
        out = []
        for d in range(self.nb):
            for n, (t, m, r) in enumerate(self.sends(d)):
                out.append(((n + 1) * self.i_cols, ("i", t, m ^ (1 << d), r)))
        for n in range((self.R - 1) * self.KT):
            out.append(((n + 1) * self.a_cols, ("a", 1 + n // self.KT, n % self.KT)))
        return [e for _, e in sorted(out, key=lambda e: e[0])]


def kernel(plan, imask, amask, i_hbm, a_hbm, o_ref, i_all, a_all, acc,
           local_sem, i_send, i_sib, i_recv, a_send, a_recv):
    p = plan
    z, c = lax.axis_index("row"), lax.axis_index("col")
    g, core = c // CORES, lax.rem(c, CORES)
    sibling = (z, g * CORES + 1 - core)

    def flip(value, mask):
        for b in range(p.nb):
            if mask >> b & 1:
                value = value + (1 << b) - (2 << b) * lax.rem(value // (1 << b), 2)
        return value

    def partner(d):
        return (z, flip(g, 1 << d) * CORES + core)

    has = {1: z < p.R - 1, -1: z > 0}

    bar = pltpu.get_barrier_semaphore()
    pl.semaphore_signal(bar, inc=1, device_id=sibling, device_id_type=MESH)
    for d in range(p.nb):
        pl.semaphore_signal(bar, inc=1, device_id=partner(d), device_id_type=MESH)
    for s in (1, -1):
        @pl.when(has[s])
        def _():
            pl.semaphore_signal(bar, inc=1, device_id=(z + s, c), device_id_type=MESH)
    ends = (z + p.R - 1) // p.R + (2 * p.R - 2 - z) // p.R
    pl.semaphore_wait(bar, 1 + p.nb + ends)

    def i_place(m, r, which):
        lanes = pl.ds(pl.multiple_of(which * p.i_cols, 128), p.i_cols)
        return i_all.at[flip(g, m), pl.ds(r * TILE, TILE), lanes]

    def i_source(m, r):
        return i_hbm.at[pl.ds(r * TILE, TILE)] if m == 0 else i_place(m, r, core)

    def i_link(d, m, r):
        return pltpu.make_async_remote_copy(
            i_source(m, r), i_place(m, r, core), i_send.at[d, m, r],
            i_recv.at[flip(g, m), core, r], device_id=partner(d), device_id_type=MESH)

    def i_cross(m, r):
        return pltpu.make_async_remote_copy(
            i_source(m, r), i_place(m, r, core), i_sib.at[m, r],
            i_recv.at[flip(g, m), core, r], device_id=sibling, device_id_type=MESH)

    def i_wait(m, r, which):
        pltpu.make_async_remote_copy(
            i_place(m, r, which), i_place(m, r, which), i_sib.at[m, r],
            i_recv.at[flip(g, m), which, r], device_id=sibling, device_id_type=MESH).wait_recv()

    def a_place(t, kt, s):
        return a_all.at[z - s * t, pl.ds(kt * TILE, TILE)]

    def a_link(t, kt, s):
        src = a_hbm.at[pl.ds(kt * TILE, TILE)] if t == 0 else a_place(t, kt, s)
        return pltpu.make_async_remote_copy(
            src, a_place(t, kt, s), a_send.at[(1 - s) // 2, t, kt],
            a_recv.at[z - s * t, kt], device_id=(z + s, c), device_id_type=MESH)

    def origin_ok(t, s):
        return z >= t if s == 1 else z + t <= p.R - 1

    for kt in range(p.KT):
        for s in (1, -1):
            @pl.when(has[s])
            def _():
                a_link(0, kt, s).start()
    own = [[(m, r) for _, m, r in p.sends(d) if m == 0] for d in range(p.nb)]
    for n in range(p.RT):
        for d in range(p.nb):
            i_link(d, *own[d][n]).start()
    for r in range(p.RT):
        i_cross(0, r).start()
    lanes = pl.ds(pl.multiple_of(core * p.i_cols, 128), p.i_cols)
    own_i = pltpu.make_async_copy(i_hbm, i_all.at[g, :, lanes], local_sem.at[0])
    own_a = pltpu.make_async_copy(a_hbm, a_all.at[z], local_sem.at[1])
    own_i.start()
    own_a.start()
    acc[...] = jnp.zeros_like(acc)

    def multiply(j, kt):
        k = j * p.KT + kt

        @pl.loop(0, p.RT)
        def _(r):
            at = pl.ds(pl.multiple_of(r * TILE, TILE), TILE)
            left = i_all[j, at, pl.ds(kt * TILE, TILE)]
            for q in range(p.QT):
                cols = pl.ds(q * TILE, TILE)
                part = jnp.dot(left, a_all[j, pl.ds(kt * TILE, TILE), cols],
                               preferred_element_type=jnp.float32)
                keep = (imask[r, k] * amask[k, q]).astype(jnp.float32)
                acc[at, cols] += keep * part

    def a_arrive(t, kt):
        for s in (1, -1):
            @pl.when(origin_ok(t, s))
            def _():
                pltpu.make_async_remote_copy(
                    a_place(t, kt, s), a_place(t, kt, s), a_send.at[0, 0, kt],
                    a_recv.at[z - s * t, kt], device_id=sibling, device_id_type=MESH).wait_recv()

                @pl.when(has[s])
                def _():
                    a_link(t, kt, s).start()

    def a_use(t, kt):
        for s in (1, -1):
            @pl.when(origin_ok(t, s))
            def _():
                multiply(z - s * t, kt)

    events = p.events()
    last_i = max(n for n, e in enumerate(events) if e[0] == "i")
    pending = []
    for n, event in enumerate(events):
        if event[0] == "a":
            _, t, kt = event
            a_arrive(t, kt)
            if n < last_i:
                pending.append((t, kt))
            else:
                a_use(t, kt)
            continue
        _, t, m, r = event
        i_wait(m, r, core)
        for u in range(t + 1, p.nb):
            i_link(p.dim(r, u), m, r).start()
        i_cross(m, r).start()
        if n == last_i:
            own_i.wait()
            own_a.wait()
            for m in range(p.G):
                for r in range(p.RT):
                    i_wait(m, r, 1 - core)
            for kt in range(p.KT):
                multiply(z, kt)
            for item in pending:
                a_use(*item)
    o_ref[...] = acc[...].astype(o_ref.dtype)

    for d in range(p.nb):
        for _, m, r in p.sends(d):
            i_link(d, m, r).wait_send()
    for m in range(p.G):
        for r in range(p.RT):
            i_cross(m, r).wait_send()
    for t in range(p.R - 1):
        for kt in range(p.KT):
            for s in (1, -1):
                @pl.when(has[s] & origin_ok(t, s))
                def _():
                    a_link(t, kt, s).wait_send()


def per_device(n_row, n_col, integrals, amplitudes, int_shape, amp_shape):
    rows, i_cols = integrals.shape
    a_rows, a_cols = amplitudes.shape
    p = Plan(n_row, n_col, rows, i_cols, a_rows, a_cols)
    dma = pltpu.SemaphoreType.DMA
    return pl.pallas_call(
        functools.partial(kernel, p),
        out_shape=jax.ShapeDtypeStruct((rows, a_cols), jnp.bfloat16),
        in_specs=[pl.BlockSpec(memory_space=pltpu.SMEM)] * 2 + [pl.BlockSpec(memory_space=pl.ANY)] * 2,
        out_specs=pl.BlockSpec(memory_space=pltpu.VMEM),
        scratch_shapes=[
            pltpu.VMEM((p.G, rows, i_cols * CORES), jnp.bfloat16),
            pltpu.VMEM((p.R, a_rows, a_cols), jnp.bfloat16),
            pltpu.VMEM((rows, a_cols), jnp.float32),
            dma((2,)),
            dma((p.nb, p.G, p.RT)),
            dma((p.G, p.RT)),
            dma((p.G, CORES, p.RT)),
            dma((2, p.R, p.KT)),
            dma((p.R, p.KT)),
        ],
        compiler_params=pltpu.CompilerParams(
            collective_id=0, has_side_effects=True, vmem_limit_bytes=60 * 2**20
        ),
    )(int_shape, amp_shape, integrals, amplitudes)


def solution(mesh):
    in_specs = (P("row", "col"), P("row", "col"), P("row", None), P(None, "col"))
    out_specs = P("row", "col")
    body = functools.partial(per_device, mesh.shape["row"], mesh.shape["col"])
    return jax.shard_map(body, mesh=mesh, in_specs=in_specs, out_specs=out_specs, check_vma=False)
```

time: 208 us -> 101 us (0.49)
  waiting for transfers between devices: 155 us -> 0 us
  Pallas kernels: 0 us -> 96.3 us
  matrix products: 14.4 us -> 0 us
  between operations: 13.5 us -> 0.01 us
  other arithmetic: 11.5 us -> 0 us
  local copies, waits for them, and re-layouts: 13.8 us -> 3.82 us
    all_gather x2 -> x0, waiting for transfers between devices: 154 us -> none  [the longest x1 88.1 us: per_device(): whole_amp = lax.all_gather(amplitudes, 'row', axis=0, tiled=True) * amp_mask]
    pallas_call x0 -> x1, Pallas kernels: none -> 96.3 us  [per_device(): pl.pallas_call(functools.partial(kernel, p), out_shape=jax.ShapeDtypeStru...]
    dot_general x1 -> x0, matrix products: 14.4 us -> none  [per_device(): total = jnp.dot(left, whole_amp, preferred_element_type=jnp.float32)]
    mul x1 -> x0, other arithmetic: 11.5 us -> none  [per_device(): left = lax.all_gather(integrals, 'col', axis=1, tiled=True) * int_mask]
    broadcast_in_dim x2 -> x0, local copies, waits for them, and re-layouts: 6.33 us -> none  [the longest x1 6.16 us: expand_shape(): jnp.repeat(jnp.repeat(shape_mask, TILE, axis=0), TILE, axis=1)]
    unnamed x9 -> x2, local copies, waits for them, and re-layouts: 7.24 us -> 3.82 us
  transfers between devices with their start and end apart: 2 -> 0, of which waited for: 2 -> 0; matrix products, arithmetic and copies ran while one was open for 10% -> 0% of each run, Pallas kernels for 0% -> 0%
where the time goes in v1:
time: 101 us; the launch traced here: 100 us
  Pallas kernels  96.3 us (95%)
  local copies, waits for them, and re-layouts  3.82 us (4%)
    pallas_call x1, Pallas kernels, per_device(): pl.pallas_call(functools.partial(kernel, p), out_shape=jax.ShapeDtypeStru...  96.3 us
    unnamed x2, local copies, waits for them, and re-layouts  3.82 us

profile of v1, /device:TPU:0, one launch (start us, length us, event | category | flops | bytes accessed | tf_op | source)
XLA Modules:
  0.0 100.1 jit_solution(17960157712310783830)
XLA Ops:
  0.0 1.4 %copy.5.amask = s32[20,2]{1,0:T(8,128)} copy(s32[20,2]{0,1:T(2,128)} %param.7) | data formatting | bytes 320 | tf_op args[3]
  1.4 96.3 %shard_map.46 = bf16[1280,512]{1,0:T(8,128)(2,1)} custom-call(s32[5,20]{1,0:T(8,128)} %imask.1, s32[20,2]{1,0:T(8,128)} %copy.5.amask, bf16[1280,640]{1,0:T(8,128)(2,1)} %i_hbm.1, bf16[1280,512]{1,0:T(8,128)(2,1)} %a_hbm.1), custom_call_target="tpu_custom_call" | custom-call | tf_op jit(solution)/shard_map/pallas_call | solution.py:214
  97.7 2.5 %copy.7 = bf16[1280,512]{1,0:T(8,128)(2,1)} copy(bf16[1280,512]{1,0:T(8,128)(2,1)} %shard_map.46) | data formatting | bytes 2621440

commit v2 on v1

--- a/solution.py
+++ b/solution.py
@@ -50,7 +50,7 @@
         return [e for _, e in sorted(out, key=lambda e: e[0])]
 
 
-def kernel(plan, imask, amask, i_hbm, a_hbm, o_ref, i_all, a_all, acc,
+def kernel(plan, imask_hbm, amask_hbm, i_hbm, a_hbm, o_ref, imask, amask, i_all, a_all, acc,
            local_sem, i_send, i_sib, i_recv, a_send, a_recv):
     p = plan
     z, c = lax.axis_index("row"), lax.axis_index("col")
@@ -128,22 +128,28 @@
     own_i = pltpu.make_async_copy(i_hbm, i_all.at[g, :, lanes], local_sem.at[0])
     own_a = pltpu.make_async_copy(a_hbm, a_all.at[z], local_sem.at[1])
     own_i.start()
+    masks = [pltpu.make_async_copy(imask_hbm, imask, local_sem.at[2]),
+             pltpu.make_async_copy(amask_hbm, amask, local_sem.at[3])]
+    for copy in masks:
+        copy.start()
     own_a.start()
     acc[...] = jnp.zeros_like(acc)
 
+    def masked_right(j, kt):
+        at = pl.ds(kt * TILE, TILE)
+        k = j * p.KT + kt
+        return [jnp.where(amask[q, k] != 0, a_all[j, at, pl.ds(q * TILE, TILE)], zero) for q in range(p.QT)]
+
+    def masked_left(j, r, kt):
+        at, cols = pl.ds(r * TILE, TILE), pl.ds(kt * TILE, TILE)
+        return jnp.where(imask[r, j * p.KT + kt] != 0, i_all[j, at, cols], zero)
+
+    zero = jnp.zeros((TILE, TILE), jnp.bfloat16)
+
     def multiply(j, kt):
-        k = j * p.KT + kt
-
-        @pl.loop(0, p.RT)
-        def _(r):
-            at = pl.ds(pl.multiple_of(r * TILE, TILE), TILE)
-            left = i_all[j, at, pl.ds(kt * TILE, TILE)]
-            for q in range(p.QT):
-                cols = pl.ds(q * TILE, TILE)
-                part = jnp.dot(left, a_all[j, pl.ds(kt * TILE, TILE), cols],
-                               preferred_element_type=jnp.float32)
-                keep = (imask[r, k] * amask[k, q]).astype(jnp.float32)
-                acc[at, cols] += keep * part
+        right = jnp.concatenate(masked_right(j, kt), axis=1)
+        left = jnp.concatenate([masked_left(j, r, kt) for r in range(p.RT)], axis=0)
+        acc[...] += jnp.dot(left, right, preferred_element_type=jnp.float32)
 
     def a_arrive(t, kt):
         for s in (1, -1):
@@ -183,6 +189,8 @@
         if n == last_i:
             own_i.wait()
             own_a.wait()
+            for copy in masks:
+                copy.wait()
             for m in range(p.G):
                 for r in range(p.RT):
                     i_wait(m, r, 1 - core)
@@ -213,14 +221,16 @@
     dma = pltpu.SemaphoreType.DMA
     return pl.pallas_call(
         functools.partial(kernel, p),
-        out_shape=jax.ShapeDtypeStruct((rows, a_cols), jnp.bfloat16),
-        in_specs=[pl.BlockSpec(memory_space=pltpu.SMEM)] * 2 + [pl.BlockSpec(memory_space=pl.ANY)] * 2,
+        out_shape=pltpu.VMEM((rows, a_cols), jnp.bfloat16),
+        in_specs=[pl.BlockSpec(memory_space=pltpu.HBM)] * 4,
         out_specs=pl.BlockSpec(memory_space=pltpu.VMEM),
         scratch_shapes=[
+            pltpu.SMEM(int_shape.shape, jnp.int32),
+            pltpu.SMEM(amp_shape.shape[::-1], jnp.int32),
             pltpu.VMEM((p.G, rows, i_cols * CORES), jnp.bfloat16),
             pltpu.VMEM((p.R, a_rows, a_cols), jnp.bfloat16),
             pltpu.VMEM((rows, a_cols), jnp.float32),
-            dma((2,)),
+            dma((4,)),
             dma((p.nb, p.G, p.RT)),
             dma((p.G, p.RT)),
             dma((p.G, CORES, p.RT)),
@@ -228,9 +238,9 @@
             dma((p.R, p.KT)),
         ],
         compiler_params=pltpu.CompilerParams(
-            collective_id=0, has_side_effects=True, vmem_limit_bytes=60 * 2**20
+            collective_id=0, has_side_effects=True, vmem_limit_bytes=56 * 2**20
         ),
-    )(int_shape, amp_shape, integrals, amplitudes)
+    )(int_shape, amp_shape.T, integrals, amplitudes)
 
 
 def solution(mesh):

time: 101 us -> 92.9 us (0.920)
  Pallas kernels: 96.3 us -> 91.7 us
  local copies, waits for them, and re-layouts: 3.82 us -> 1.06 us
    pallas_call x1, Pallas kernels: 96.3 us -> 91.7 us  [per_device(): pl.pallas_call(functools.partial(kernel, p), out_shape=pltpu.VMEM((rows,...]
    unnamed x2 -> x1, local copies, waits for them, and re-layouts: 3.82 us -> 1.06 us
where the time goes in v2:
time: 92.9 us; the launch traced here: 92.8 us
  Pallas kernels  91.7 us (99%)
  local copies, waits for them, and re-layouts  1.06 us (1%)
    pallas_call x1, Pallas kernels, per_device(): pl.pallas_call(functools.partial(kernel, p), out_shape=pltpu.VMEM((rows,...  91.7 us

profile of v2, /device:TPU:0, one launch (start us, length us, event | category | flops | bytes accessed | tf_op | source)
XLA Modules:
  0.0 92.8 jit_solution(13287273226814171756)
XLA Ops:
  0.0 91.7 %shard_map.46 = bf16[1280,512]{1,0:T(8,128)(2,1)S(1)} custom-call(s32[5,20]{1,0:T(8,128)} %imask_hbm.1, s32[2,20]{1,0:T(2,128)} %bitcast.1, bf16[1280,640]{1,0:T(8,128)(2,1)} %i_hbm.1, bf16[1280,512]{1,0:T(8,128)(2,1)} %a_hbm.1), custom_call_target="tpu_custom_call" | custom-call | tf_op jit(solution)/shard_map/pallas_call | solution.py:222
  91.7 1.1 %copy.6 = bf16[1280,512]{1,0:T(8,128)(2,1)} copy(bf16[1280,512]{1,0:T(8,128)(2,1)S(1)} %shard_map.46) | data formatting | bytes 2621440

commit v3 on v2

--- a/solution.py
+++ b/solution.py
@@ -146,10 +146,13 @@
 
     zero = jnp.zeros((TILE, TILE), jnp.bfloat16)
 
-    def multiply(j, kt):
+    def product(j, kt):
         right = jnp.concatenate(masked_right(j, kt), axis=1)
         left = jnp.concatenate([masked_left(j, r, kt) for r in range(p.RT)], axis=0)
-        acc[...] += jnp.dot(left, right, preferred_element_type=jnp.float32)
+        return jnp.dot(left, right, preferred_element_type=jnp.float32)
+
+    def multiply(j, kt):
+        acc[...] += product(j, kt)
 
     def a_arrive(t, kt):
         for s in (1, -1):
@@ -167,7 +170,10 @@
         for s in (1, -1):
             @pl.when(origin_ok(t, s))
             def _():
-                multiply(z - s * t, kt)
+                if (t, kt) == (p.R - 1, p.KT - 1):
+                    o_ref[...] = (acc[...] + product(z - s * t, kt)).astype(o_ref.dtype)
+                else:
+                    multiply(z - s * t, kt)
 
     events = p.events()
     last_i = max(n for n, e in enumerate(events) if e[0] == "i")
@@ -198,7 +204,10 @@
                 multiply(z, kt)
             for item in pending:
                 a_use(*item)
-    o_ref[...] = acc[...].astype(o_ref.dtype)
+
+    @pl.when((z > 0) & (z < p.R - 1))
+    def _():
+        o_ref[...] = acc[...].astype(o_ref.dtype)
 
     for d in range(p.nb):
         for _, m, r in p.sends(d):

time: 92.9 us -> 92.8 us (level)
  no operation moved by 1% of the time
where the time goes in v3:
time: 92.8 us; the launch traced here: 92.7 us
  Pallas kernels  91.6 us (99%)
  local copies, waits for them, and re-layouts  1.06 us (1%)
    pallas_call x1, Pallas kernels, per_device(): pl.pallas_call(functools.partial(kernel, p), out_shape=pltpu.VMEM((rows,...  91.6 us

profile of v3, /device:TPU:0, one launch (start us, length us, event | category | flops | bytes accessed | tf_op | source)
XLA Modules:
  0.0 92.7 jit_solution(6456712174957742774)
XLA Ops:
  0.0 91.6 %shard_map.46 = bf16[1280,512]{1,0:T(8,128)(2,1)S(1)} custom-call(s32[5,20]{1,0:T(8,128)} %imask_hbm.1, s32[2,20]{1,0:T(2,128)} %bitcast.1, bf16[1280,640]{1,0:T(8,128)(2,1)} %i_hbm.1, bf16[1280,512]{1,0:T(8,128)(2,1)} %a_hbm.1), custom_call_target="tpu_custom_call" | custom-call | tf_op jit(solution)/shard_map/pallas_call | solution.py:231
  91.6 1.1 %copy.6 = bf16[1280,512]{1,0:T(8,128)(2,1)} copy(bf16[1280,512]{1,0:T(8,128)(2,1)S(1)} %shard_map.46) | data formatting | bytes 2621440
